TPU v7x, 256 devices: a whole 4x4x8 slice. The times are simulated.
256 devices in a mesh: dp: 16 (over y_hi, z), mx: 8 (over x, core), my: 2 (over y_lo).
Axes of the slice: x: 4, y: 4 (y_hi: 2, y_lo: 2; y = y_hi * 2 + y_lo), z: 8, core: 2. Of those that a mesh axis runs over, the one named last changes fastest.
Arguments:
- inputs: bfloat16 [4096, 6144], P('dp', 'mx'), may hold values from -300 to 300
- ln_gain: float32 [6144], P('mx'), may hold values from 0.5 to 1.5
- w_qkv: bfloat16 [3, 6144, 4096], P(None, 'mx', 'my'), may hold values from -1 to 1
- qk_gain: float32 [2, 32, 128], P(None, ('my', 'mx')), may hold values from 0 to 8, as said below
- d_out: bfloat16 [4096, 4096], P('dp', ('my', 'mx')), may hold values from -110 to 110
Outputs:
- input_grad: bfloat16 [4096, 6144], P('dp', 'mx')
- w_grad: bfloat16 [3, 6144, 4096], P(None, ('mx', 'dp'), 'my')
- ln_gain_grad: float32 [6144], P('mx')
- qk_gain_grad: float32 [2, 32, 128], P(None, ('my', 'mx'))
Inputs may be any that keep to these rules, and one draw needn't show every extreme that they name: `qk_gain`: positive.
All inputs are finite; a program needn't handle non-finite values.
Results may differ from a plain program's by a relative error of at most 0.015.
The roundings to bfloat16 on the way count: a program that leaves them out, or rounds other values in their place, can miss the bound.
Values may be sent and summed in bfloat16 or wider, within the bound.
A program may use at most 128 MiB of HBM per device.

v0:
```python
import math
import jax
import jax.numpy as jnp
from jax import lax
from jax.sharding import PartitionSpec as P

PATCH = 256
epsilon = 1e-06


def head_norm(values):
    average = jnp.mean(values, axis=-1, keepdims=True)
    spread = jnp.mean(values * values, axis=-1, keepdims=True) - average * average
    inv_scale = lax.rsqrt(spread + epsilon)
    return ((values - average) * inv_scale, inv_scale)


def norm_back(d_normed, normed, inv_scale, gain_row):
    d_hat = d_normed * gain_row
    return inv_scale * (
        d_hat
        - jnp.mean(d_hat, axis=-1, keepdims=True)
        - normed * jnp.mean(d_hat * normed, axis=-1, keepdims=True)
    )


def body(inputs, ln_gain, w_qkv, qk_gain, d_out):
    token_rows = inputs.shape[0]
    width_local = inputs.shape[1]
    width = width_local * lax.axis_size("mx")
    widened = inputs.astype(jnp.float32)
    totals = lax.psum((jnp.sum(widened, axis=1), jnp.sum(widened * widened, axis=1)), "mx")
    average = totals[0][:, None] / width
    spread = totals[1][:, None] / width - average * average
    inv_scale = lax.rsqrt(spread + epsilon)
    normed = (widened - average) * inv_scale
    scaled = (normed * ln_gain[None, :]).astype(jnp.bfloat16)
    local_heads = qk_gain.shape[1]
    head_size = qk_gain.shape[2]
    group_heads = w_qkv.shape[2] // head_size
    weights = w_qkv.reshape(3, width_local, group_heads, head_size)
    projected = lax.psum_scatter(
        jnp.einsum("td,sdhe->hste", scaled, weights, preferred_element_type=jnp.float32),
        "mx",
        scatter_dimension=0,
        tiled=True,
    ).astype(jnp.bfloat16)
    images = token_rows // PATCH
    shaped = projected.reshape(local_heads, 3, images, PATCH, head_size)
    q_hat, q_inv = head_norm(shaped[:, 0].astype(jnp.float32))
    k_hat, k_inv = head_norm(shaped[:, 1].astype(jnp.float32))
    values = shaped[:, 2]
    q_gain = qk_gain[0][:, None, None, :]
    k_gain = qk_gain[1][:, None, None, :]
    q_normed = (q_hat * q_gain).astype(jnp.bfloat16)
    k_normed = (k_hat * k_gain).astype(jnp.bfloat16)
    factor = 1.0 / math.sqrt(head_size)
    scores = (
        jnp.einsum("hipe,hiqe->hipq", q_normed, k_normed, preferred_element_type=jnp.float32)
        * factor
    )
    row_max = jnp.max(scores, axis=-1, keepdims=True)
    exponent = jnp.exp(scores - row_max)
    probabilities = exponent / jnp.sum(exponent, axis=-1, keepdims=True)
    probs_low = probabilities.astype(jnp.bfloat16)
    grad_heads = (
        d_out.reshape(token_rows, local_heads, head_size)
        .transpose(1, 0, 2)
        .reshape(local_heads, images, PATCH, head_size)
    )
    d_values = jnp.einsum(
        "hipq,hipe->hiqe", probs_low, grad_heads, preferred_element_type=jnp.float32
    ).astype(jnp.bfloat16)
    d_probs = jnp.einsum("hipe,hiqe->hipq", grad_heads, values, preferred_element_type=jnp.float32)
    row_delta = jnp.sum(probabilities * d_probs, axis=-1, keepdims=True)
    d_scores = (probabilities * (d_probs - row_delta) * factor).astype(jnp.bfloat16)
    d_qn = jnp.einsum("hipq,hiqe->hipe", d_scores, k_normed, preferred_element_type=jnp.float32)
    d_kn = jnp.einsum("hipq,hipe->hiqe", d_scores, q_normed, preferred_element_type=jnp.float32)
    head_gain_part = jnp.stack(
        [jnp.sum(d_qn * q_hat, axis=(1, 2)), jnp.sum(d_kn * k_hat, axis=(1, 2))]
    )
    d_query = norm_back(d_qn, q_hat, q_inv, q_gain).astype(jnp.bfloat16)
    d_key = norm_back(d_kn, k_hat, k_inv, k_gain).astype(jnp.bfloat16)

    def head_rows(grads):
        return grads.reshape(local_heads, token_rows, head_size)

    block_rows = width_local // lax.axis_size("dp")
    stacked = jnp.stack([head_rows(d_query), head_rows(d_key), head_rows(d_values)], axis=1)
    gathered = lax.all_gather(stacked, "mx", axis=0, tiled=True)
    d_scaled = jnp.einsum("hste,sdhe->td", gathered, weights, preferred_element_type=jnp.float32)
    feature_part = scaled
    w_rows = lax.psum_scatter(
        jnp.einsum(
            "td,hste->dshe", feature_part, gathered, preferred_element_type=jnp.float32
        ).astype(jnp.bfloat16),
        "dp",
        scatter_dimension=0,
        tiled=True,
    ).astype(jnp.float32)
    w_grad = (
        w_rows.reshape(block_rows, 3, group_heads * head_size)
        .transpose(1, 0, 2)
        .astype(jnp.bfloat16)
    )
    gain_row = ln_gain[None, :]
    d_rows = lax.psum(d_scaled.astype(jnp.bfloat16), "my").astype(jnp.float32)
    d_hat = d_rows * gain_row
    stat_sums = lax.psum((jnp.sum(d_hat, axis=1), jnp.sum(d_hat * normed, axis=1)), "mx")
    sum_first = stat_sums[0]
    sum_second = stat_sums[1]
    result_rows = (
        inv_scale * (d_hat - sum_first[:, None] / width - normed * sum_second[:, None] / width)
    ).astype(jnp.bfloat16)
    feature_part = jnp.sum(d_rows * normed, axis=0)
    head_total, feature_total = lax.psum((head_gain_part, feature_part), "dp")
    return (result_rows, w_grad, feature_total, head_total)


def solution(mesh):
    in_specs = (
        P("dp", "mx"),
        P("mx"),
        P(None, "mx", "my"),
        P(None, ("my", "mx"), None),
        P("dp", ("my", "mx")),
    )
    out_specs = (P("dp", "mx"), P(None, ("mx", "dp"), "my"), P("mx"), P(None, ("my", "mx"), None))
    return jax.shard_map(body, mesh=mesh, in_specs=in_specs, out_specs=out_specs, check_vma=False)
```

profile of v0, /device:TPU:2, one launch (start us, length us, event | category | flops | bytes accessed | tf_op | source)
XLA Modules:
  0.0 439.1 jit_solution(7487721284132833700)
XLA Ops:
  7.2 0.0 copy-start
  7.2 0.0 all-gather.2.cloned.1.call-start
  7.2 0.7 slice_bitcast_fusion.3
  7.9 1.2 fusion.44
  9.1 11.7 %all-reduce.3 = (f32[256]{0:T(256)S(1)}, f32[256]{0:T(256)S(1)}) all-reduce(f32[256]{0:T(256)S(1)} %get-tuple-element.18, f32[256]{0:T(256)S(1)} %get-tuple-element.17), channel_id=1, replica_groups=mesh['dp'=16,'mx'=8,'my'=2] {'mx'}, use_global_device_ids=true, to_apply=%region_3.0 | all-reduce | flops 512 | bytes 4096 | tf_op jit(solution)/shard_map/psum | solution.py:32
  20.8 9.2 %fusion.10 = f32[16,3,256,128]{3,2,0,1:T(8,128)} fusion(bf16[256,768]{1,0:T(8,128)(2,1)} %param.5, f32[768]{0:T(1024)} %param.6, f32[256]{0:T(256)S(1)} %get-tuple-element.36, f32[256]{0:T(256)S(1)} %get-tuple-element.35, bf16[3,768,2048]{2,1,0:T(8,128)(2,1)} %param.7), kind=kOutput, calls=%fused_computation.11 | convolution fusion | flops 2416902144 | bytes 16126976 | tf_op jit(solution)/shard_map/td,sdhe->hste/dot_general | solution.py:43
  30.0 0.0 copy-start.5
  30.0 71.0 %all-reduce.8 = bf16[16,3,256,128]{3,2,0,1:T(8,128)(2,1)S(1)} all-reduce(f32[16,3,256,128]{3,2,0,1:T(8,128)} %fusion.10), channel_id=2, replica_groups=mesh['dp'=16,'mx'=8,'my'=2] {'mx'}, use_global_device_ids=true, to_apply=%region_4.0.clone | all-reduce | flops 1572864 | bytes 9437184
  101.0 0.0 copy-done.5
  101.0 0.6 dynamic-slice
  102.3 0.0 copy-start.2
  102.3 0.3 fusion.52
  102.6 0.4 copy-done.2
  103.1 0.0 copy-done
  103.1 0.2 convolution_bitcast_fusion
  103.3 0.0 copy-start.3
  103.3 1.6 fusion.109
  104.9 0.2 fusion.29
  105.2 1.3 fusion.30
  106.5 2.1 fusion.64
  108.6 0.0 copy-done.3
  108.6 0.6 fusion.84
  109.3 0.8 pad_maximum_fusion
  110.1 0.0 all-gather.2.cloned.1.call-update
  110.1 0.0 copy-start.1
  110.1 0.0 copy-start.4
  110.1 0.0 all-reduce.7.cloned.1.call-start
  110.2 33.7 %all-gather.2.cloned.1.call-done = bf16[16,3,256,128]{3,2,0,1:T(8,128)(2,1)} async-done(((bf16[2,3,256,128]{3,2,0,1:T(8,128)(2,1)}), bf16[16,3,256,128]{3,2,0,1:T(8,128)(2,1)}) %all-gather.2.cloned.1.call-update) | async-done | bytes 3145744 | tf_op jit(solution)/shard_map/all_gather | solution.py:90
  143.8 8.0 %fusion.19 = bf16[256,768]{1,0:T(8,128)(2,1)} fusion(bf16[16,3,256,128]{3,2,0,1:T(8,128)(2,1)} %all-gather.2.cloned.1.call-done, bf16[3,768,2048]{2,1,0:T(8,128)(2,1)} %param.7), kind=kOutput, calls=%fused_computation.14 | convolution fusion | flops 2416115712 | bytes 12976128 | tf_op jit(solution)/shard_map/hste,sdhe->td/dot_general | solution.py:91
  151.8 0.0 all-reduce.7.cloned.1.call-update
  151.8 0.2 reduce-scatter.5.cloned.1.call-start
  152.1 0.0 copy-done.1
  152.1 0.0 copy-done.4
  152.1 8.3 %convert_bitcast_fusion = bf16[768,3,16,128]{0,3,1,2:T(8,128)(2,1)} fusion(bf16[16,3,256,128]{3,2,0,1:T(8,128)(2,1)} %all-gather.2.cloned.1.call-done, bf16[256,768]{1,0:T(8,128)(2,1)S(1)} %copy-done.1, f32[768]{0:T(1024)S(1)} %copy-done.4, f32[256]{0:T(256)S(1)} %get-tuple-element.36, f32[256]{0:T(256)S(1)} %get-tuple-element.35), kind=kOutput, calls=%fused_computation.8 | convolution fusion | flops 2421620736 | bytes 12981248 | tf_op jit(solution)/shard_map/td,hste->dshe/dot_general | solution.py:94
  160.4 13.2 %copy.49 = bf16[768,3,16,128]{3,2,1,0:T(8,128)(2,1)} copy(bf16[768,3,16,128]{0,3,1,2:T(8,128)(2,1)} %convert_bitcast_fusion) | data formatting | bytes 18874368 | tf_op jit(solution)/shard_map/convert_element_type | solution.py:96
  173.6 0.0 reduce-scatter.5.cloned.1.call-update
  173.7 16.8 %all-reduce.7.cloned.1.call-done = bf16[256,768]{1,0:T(8,128)(2,1)} async-done(((bf16[256,768]{1,0:T(8,128)(2,1)}), bf16[256,768]{1,0:T(8,128)(2,1)}) %all-reduce.7.cloned.1.call-update) | async-done | bytes 393232 | tf_op jit(solution)/shard_map/psum | solution.py:107
  190.5 1.4 fusion.43
  191.9 11.5 %all-reduce.2 = (f32[256]{0:T(256)S(1)}, f32[256]{0:T(256)S(1)}) all-reduce(f32[256]{0:T(256)S(1)} %get-tuple-element.5, f32[256]{0:T(256)S(1)} %get-tuple-element.10), channel_id=1, replica_groups=mesh['dp'=16,'mx'=8,'my'=2] {'mx'}, use_global_device_ids=true, to_apply=%region_20.0 | all-reduce | flops 512 | bytes 4096 | tf_op jit(solution)/shard_map/psum | solution.py:109
  203.4 43.4 %all-reduce.1 = (f32[768]{0:T(1024)}, f32[2,2,128]{2,1,0:T(2,128)}) all-reduce(f32[768]{0:T(1024)S(1)} %get-tuple-element.4, f32[2,2,128]{2,1,0:T(2,128)S(1)} %pad_maximum_fusion.1), channel_id=1, replica_groups=mesh['dp'=16,'mx'=8,'my'=2] {'dp'}, use_global_device_ids=true, to_apply=%region_23.0 | all-reduce | flops 1280 | bytes 10240 | tf_op jit(solution)/shard_map/psum | solution.py:116
  246.8 2.1 fusion.41
  248.9 181.5 %reduce-scatter.5.cloned.1.call-done = bf16[48,3,16,128]{3,2,1,0:T(8,128)(2,1)} async-done(((bf16[768,3,16,128]{3,2,1,0:T(8,128)(2,1)}), bf16[48,3,16,128]{3,2,1,0:T(8,128)(2,1)}) %reduce-scatter.5.cloned.1.call-update) | async-done | bytes 589840 | tf_op jit(solution)/shard_map/reduce_scatter | solution.py:93
  430.4 1.2 copy.50
  431.6 1.1 convert_element_type.144
  (9 shorter events, 0.1 us)
Async XLA Ops:
  7.2 95.9 %copy-start = (bf16[256,256]{1,0:T(8,128)(2,1)S(1)}, bf16[256,256]{1,0:T(8,128)(2,1)}, u32[]{:S(2)}) copy-start(bf16[256,256]{1,0:T(8,128)(2,1)} %param.9) | copy-start | bytes 393220
  7.2 136.6 %all-gather.2.cloned.1.call-start = ((), (), s32[]{:S(2)}) async-start(), calls=%async_computation.1 | async-start | bytes 3538944 | tf_op jit(solution)/shard_map/all_gather | solution.py:90
  30.0 71.0 %copy-start.5 = (u32[256]{0:T(256)S(1)}, u32[256]{0:T(256)}, u32[]{:S(2)}) copy-start(u32[256]{0:T(256)} %constant.29) | copy-start | bytes 3076
  102.3 0.7 copy-start.2
  103.3 5.3 %copy-start.3 = (bf16[2,3,1,256,128]{4,3,0,2,1:T(8,128)(2,1)S(1)}, bf16[2,3,1,256,128]{4,3,0,2,1:T(8,128)(2,1)}, u32[]{:S(2)}) copy-start(bf16[2,3,1,256,128]{4,3,0,2,1:T(8,128)(2,1)} %copy-done.2) | copy-start | bytes 1179652
  110.1 42.0 %copy-start.1 = (bf16[256,768]{1,0:T(8,128)(2,1)S(1)}, bf16[256,768]{1,0:T(8,128)(2,1)}, u32[]{:S(2)}) copy-start(bf16[256,768]{1,0:T(8,128)(2,1)} %param.5) | copy-start | bytes 1179652
  110.1 42.0 %copy-start.4 = (f32[768]{0:T(1024)S(1)}, f32[768]{0:T(1024)}, u32[]{:S(2)}) copy-start(f32[768]{0:T(1024)} %param.6) | copy-start | bytes 9220
  110.1 80.4 %all-reduce.7.cloned.1.call-start = ((), (), s32[]{:S(2)}) async-start(), calls=%async_computation.2 | async-start | bytes 786432 | tf_op jit(solution)/shard_map/psum | solution.py:107
  151.8 278.5 %reduce-scatter.5.cloned.1.call-start = ((), (), s32[]{:S(2)}) async-start(), calls=%async_computation.3 | async-start | bytes 10027008 | tf_op jit(solution)/shard_map/reduce_scatter | solution.py:93
Sparse Core Ops, SparseCore 0:
  110.2 33.5 all-gather.1
  152.0 38.4 all-reduce.6
  194.7 235.6 reduce-scatter.4
where the time goes:
time: 440 us; the launch traced here: 439 us
  waiting for transfers between devices  232 us (53%)
  blocking collectives  138 us (31%)
  matrix products  31 us (7%)
  local copies, waits for them, and re-layouts  17.3 us (4%)
  between operations  14.6 us (3%)
  other arithmetic  6.45 us (1%)
    reduce_scatter x1, waiting for transfers between devices, body(): lax.psum_scatter(jnp.einsum('td,hste->dshe', feature_part, gathered, pref...  181 us
    unnamed x1, blocking collectives  71 us
    psum x1, blocking collectives, body(): head_total, feature_total = lax.psum((head_gain_part, feature_part), 'dp')  43.4 us
    all_gather x1, waiting for transfers between devices, body(): gathered = lax.all_gather(stacked, 'mx', axis=0, tiled=True)  33.7 us
    psum x1, waiting for transfers between devices, body(): d_rows = lax.psum(d_scaled.astype(jnp.bfloat16), 'my').astype(jnp.float32)  16.8 us
    convert_element_type x1, local copies, waits for them, and re-layouts, body(): w_rows = lax.psum_scatter(jnp.einsum('td,hste->dshe', feature_part, gathe...  13.2 us
    psum x1, blocking collectives, body(): lax.psum((jnp.sum(widened, axis=1), jnp.sum(widened * widened, axis=1)),...  11.7 us
    psum x1, blocking collectives, body(): lax.psum((jnp.sum(d_hat, axis=1), jnp.sum(d_hat * normed, axis=1)), 'mx')  11.5 us
  transfers between devices with their start and end apart: 3, of which 3 were waited for; matrix products, arithmetic and copies ran while one was open for 6% of the time, Pallas kernels for 0%

commit v1 on v0

--- a/solution.py
+++ b/solution.py
@@ -87,7 +87,16 @@
 
     block_rows = width_local // lax.axis_size("dp")
     stacked = jnp.stack([head_rows(d_query), head_rows(d_key), head_rows(d_values)], axis=1)
-    gathered = lax.all_gather(stacked, "mx", axis=0, tiled=True)
+    ways = lax.axis_size("mx")
+    up = [(d, (d + 1) % ways) for d in range(ways)]
+    down = [(d, (d - 1) % ways) for d in range(ways)]
+    earlier, later = ([stacked], [stacked])
+    for _ in range(ways // 2):
+        earlier.append(lax.ppermute(earlier[-1], "mx", up))
+    for _ in range((ways - 1) // 2):
+        later.append(lax.ppermute(later[-1], "mx", down))
+    line = jnp.concatenate([*earlier[::-1], *later[1:]], axis=0)
+    gathered = jnp.roll(line, (lax.axis_index("mx") - ways // 2) * stacked.shape[0], axis=0)
     d_scaled = jnp.einsum("hste,sdhe->td", gathered, weights, preferred_element_type=jnp.float32)
     feature_part = scaled
     w_rows = lax.psum_scatter(

time: 440 us -> 428 us (0.973)
  waiting for transfers between devices: 232 us -> 211 us
  starting transfers between devices: 0.3 us -> 5.97 us
    all_gather x1 -> x0, waiting for transfers between devices: 33.7 us -> none  [body(): gathered = lax.all_gather(stacked, 'mx', axis=0, tiled=True)]
    reduce_scatter x1, waiting for transfers between devices: 181 us -> 155 us  [body(): lax.psum_scatter(jnp.einsum('td,hste->dshe', feature_part, gathered, pref...]
    ppermute x0 -> x7, waiting for transfers between devices: none -> 23.1 us  [the longest x4 23 us: body(): earlier.append(lax.ppermute(earlier[-1], 'mx', up))]
    psum x1, waiting for transfers between devices: 16.8 us -> 32.4 us  [body(): d_rows = lax.psum(d_scaled.astype(jnp.bfloat16), 'my').astype(jnp.float32)]
    ppermute x0 -> x7, starting transfers between devices: none -> 5.71 us  [the longest x3 5.68 us: body(): later.append(lax.ppermute(later[-1], 'mx', down))]
  transfers between devices with their start and end apart: 3 -> 9, of which waited for: 3 -> 7; matrix products, arithmetic and copies ran while one was open for 6% -> 6% of each run, Pallas kernels for 0% -> 0%
where the time goes in v1:
time: 428 us; the launch traced here: 427 us
  waiting for transfers between devices  211 us (49%)
  blocking collectives  138 us (32%)
  matrix products  29.2 us (7%)
  local copies, waits for them, and re-layouts  20.6 us (5%)
  between operations  16.5 us (4%)
  starting transfers between devices  5.97 us (1%)
  other arithmetic  5.82 us (1%)
    reduce_scatter x1, waiting for transfers between devices, body(): lax.psum_scatter(jnp.einsum('td,hste->dshe', feature_part, gathered, pref...  155 us
    unnamed x1, blocking collectives  71 us
    psum x1, blocking collectives, body(): head_total, feature_total = lax.psum((head_gain_part, feature_part), 'dp')  43.3 us
    psum x1, waiting for transfers between devices, body(): d_rows = lax.psum(d_scaled.astype(jnp.bfloat16), 'my').astype(jnp.float32)  32.4 us
    ppermute x4, waiting for transfers between devices, body(): earlier.append(lax.ppermute(earlier[-1], 'mx', up))  23 us
    convert_element_type x1, local copies, waits for them, and re-layouts, body(): w_rows = lax.psum_scatter(jnp.einsum('td,hste->dshe', feature_part, gathe...  13.2 us
    psum x1, blocking collectives, body(): lax.psum((jnp.sum(d_hat, axis=1), jnp.sum(d_hat * normed, axis=1)), 'mx')  11.9 us
    psum x1, blocking collectives, body(): lax.psum((jnp.sum(widened, axis=1), jnp.sum(widened * widened, axis=1)),...  11.7 us
  transfers between devices with their start and end apart: 9, of which 7 were waited for; matrix products, arithmetic and copies ran while one was open for 6% of the time, Pallas kernels for 0%

profile of v1, /device:TPU:2, one launch (start us, length us, event | category | flops | bytes accessed | tf_op | source)
XLA Modules:
  0.0 426.9 jit_solution(9874352834875479448)
XLA Ops:
  8.1 0.7 slice_bitcast_fusion.3
  8.8 1.2 fusion.44
  9.9 11.7 %all-reduce.3 = (f32[256]{0:T(256)S(1)}, f32[256]{0:T(256)S(1)}) all-reduce(f32[256]{0:T(256)S(1)} %get-tuple-element.18, f32[256]{0:T(256)S(1)} %get-tuple-element.17), channel_id=1, replica_groups=mesh['dp'=16,'mx'=8,'my'=2] {'mx'}, use_global_device_ids=true, to_apply=%region_3.0 | all-reduce | flops 512 | bytes 4096 | tf_op jit(solution)/shard_map/psum | solution.py:32
  21.6 9.2 %fusion.10 = f32[16,3,256,128]{3,2,0,1:T(8,128)} fusion(bf16[256,768]{1,0:T(8,128)(2,1)} %param.5, f32[768]{0:T(1024)} %param.6, f32[256]{0:T(256)S(1)} %get-tuple-element.36, f32[256]{0:T(256)S(1)} %get-tuple-element.35, bf16[3,768,2048]{2,1,0:T(8,128)(2,1)} %param.7), kind=kOutput, calls=%fused_computation.11 | convolution fusion | flops 2416902144 | bytes 16126976 | tf_op jit(solution)/shard_map/td,sdhe->hste/dot_general | solution.py:43
  30.8 71.0 %all-reduce.8 = bf16[16,3,256,128]{3,2,0,1:T(8,128)(2,1)S(1)} all-reduce(f32[16,3,256,128]{3,2,0,1:T(8,128)} %fusion.10), channel_id=2, replica_groups=mesh['dp'=16,'mx'=8,'my'=2] {'mx'}, use_global_device_ids=true, to_apply=%region_4.0.clone | all-reduce | flops 1572864 | bytes 9437184
  101.9 0.6 dynamic-slice
  103.2 0.3 fusion.52
  103.5 0.4 copy-done.2
  103.9 0.2 convolution_bitcast_fusion
  104.2 1.6 fusion.109
  105.8 0.2 fusion.29
  106.0 1.3 fusion.30
  107.3 1.0 fusion.64
  108.4 0.6 fusion.84
  109.1 7.2 %collective-permute-done = bf16[2,3,256,128]{3,2,0,1:T(8,128)(2,1)S(1)} collective-permute-done((bf16[2,3,256,128]{3,2,0,1:T(8,128)(2,1)S(1)}, bf16[2,3,256,128]{3,2,0,1:T(8,128)(2,1)S(1)}, u32[]{:S(2)}, u32[]{:S(2)}) %collective-permute-start) | collective-permute-done | bytes 393248 | tf_op jit(solution)/shard_map/ppermute | solution.py:95
  116.3 1.7 collective-permute-start.4
  118.0 5.5 %collective-permute-done.1 = bf16[2,3,256,128]{3,2,0,1:T(8,128)(2,1)S(1)} collective-permute-done((bf16[2,3,256,128]{3,2,0,1:T(8,128)(2,1)S(1)}, bf16[2,3,256,128]{3,2,0,1:T(8,128)(2,1)S(1)}, u32[]{:S(2)}, u32[]{:S(2)}) %collective-permute-start.1) | collective-permute-done | bytes 393248 | tf_op jit(solution)/shard_map/ppermute | solution.py:95
  123.5 2.0 collective-permute-start.5
  125.5 5.2 %collective-permute-done.2 = bf16[2,3,256,128]{3,2,0,1:T(8,128)(2,1)S(1)} collective-permute-done((bf16[2,3,256,128]{3,2,0,1:T(8,128)(2,1)S(1)}, bf16[2,3,256,128]{3,2,0,1:T(8,128)(2,1)S(1)}, u32[]{:S(2)}, u32[]{:S(2)}) %collective-permute-start.2) | collective-permute-done | bytes 393248 | tf_op jit(solution)/shard_map/ppermute | solution.py:95
  130.7 0.1 collective-permute-done.5
  130.8 1.9 collective-permute-start.6
  132.7 5.2 %collective-permute-done.3 = bf16[2,3,256,128]{3,2,0,1:T(8,128)(2,1)S(1)} collective-permute-done((bf16[2,3,256,128]{3,2,0,1:T(8,128)(2,1)S(1)}, bf16[2,3,256,128]{3,2,0,1:T(8,128)(2,1)S(1)}, u32[]{:S(2)}, u32[]{:S(2)}) %collective-permute-start.3) | collective-permute-done | bytes 393248 | tf_op jit(solution)/shard_map/ppermute | solution.py:95
  137.9 0.1 constant_dynamic-update-slice_fusion.14
  138.1 0.1 constant_dynamic-update-slice_fusion.12
  138.1 0.1 constant_dynamic-update-slice_fusion.11
  138.2 0.1 constant_dynamic-update-slice_fusion.10
  138.2 0.1 constant_dynamic-update-slice_fusion.9
  138.3 0.1 constant_dynamic-update-slice_fusion.8
  138.4 0.1 constant_dynamic-update-slice_fusion.7
  138.4 0.1 constant_dynamic-update-slice_fusion.6
  138.5 0.1 constant_dynamic-update-slice_fusion.5
  138.6 0.1 constant_dynamic-update-slice_fusion.4
  138.6 0.1 constant_dynamic-update-slice_fusion.3
  138.7 0.1 constant_dynamic-update-slice_fusion.2
  138.7 0.1 constant_dynamic-update-slice_fusion.1
  138.9 2.7 copy-done.4
  141.5 7.3 %fusion.19 = bf16[256,768]{1,0:T(8,128)(2,1)} fusion(bf16[3,768,2048]{2,1,0:T(8,128)(2,1)} %param.7, bf16[32,3,256,128]{3,2,0,1:T(8,128)(2,1)S(1)} %constant_dynamic-update-slice_fusion, s32[]{:T(128)S(6)} %select_n.14), kind=kOutput, calls=%fused_computation.14 | convolution fusion | flops 2416115712 | bytes 12976132 | tf_op jit(solution)/shard_map/hste,sdhe->td/dot_general | solution.py:100
  148.8 0.2 reduce-scatter.5.cloned.1.call-start
  149.1 8.3 %convert_bitcast_fusion = bf16[768,3,16,128]{0,3,1,2:T(8,128)(2,1)} fusion(bf16[256,768]{1,0:T(8,128)(2,1)S(1)} %copy-done.1, f32[768]{0:T(1024)S(1)} %copy-done.5, f32[256]{0:T(256)S(1)} %get-tuple-element.36, f32[256]{0:T(256)S(1)} %get-tuple-element.35, bf16[32,3,256,128]{3,2,0,1:T(8,128)(2,1)} %copy-done.4, s32[]{:T(128)S(6)} %select_n.14), kind=kOutput, calls=%fused_computation.8 | convolution fusion | flops 2421620736 | bytes 12981252 | tf_op jit(solution)/shard_map/td,hste->dshe/dot_general | solution.py:103
  157.4 13.2 %copy.49 = bf16[768,3,16,128]{3,2,1,0:T(8,128)(2,1)} copy(bf16[768,3,16,128]{0,3,1,2:T(8,128)(2,1)} %convert_bitcast_fusion) | data formatting | bytes 18874368 | tf_op jit(solution)/shard_map/convert_element_type | solution.py:105
  170.7 32.4 %all-reduce.7.cloned.1.call-done = bf16[256,768]{1,0:T(8,128)(2,1)} async-done(((bf16[256,768]{1,0:T(8,128)(2,1)}), bf16[256,768]{1,0:T(8,128)(2,1)}) %all-reduce.7.cloned.1.call-update) | async-done | bytes 393232 | tf_op jit(solution)/shard_map/psum | solution.py:116
  203.0 1.5 fusion.43
  204.5 11.9 %all-reduce.2 = (f32[256]{0:T(256)S(1)}, f32[256]{0:T(256)S(1)}) all-reduce(f32[256]{0:T(256)S(1)} %get-tuple-element.5, f32[256]{0:T(256)S(1)} %get-tuple-element.10), channel_id=1, replica_groups=mesh['dp'=16,'mx'=8,'my'=2] {'mx'}, use_global_device_ids=true, to_apply=%region_20.21 | all-reduce | flops 512 | bytes 4096 | tf_op jit(solution)/shard_map/psum | solution.py:118
  216.3 43.3 %all-reduce.1 = (f32[768]{0:T(1024)}, f32[2,2,128]{2,1,0:T(2,128)}) all-reduce(f32[768]{0:T(1024)S(1)} %get-tuple-element.4, f32[2,2,128]{2,1,0:T(2,128)S(1)} %pad_maximum_fusion.1), channel_id=1, replica_groups=mesh['dp'=16,'mx'=8,'my'=2] {'dp'}, use_global_device_ids=true, to_apply=%region_23.24 | all-reduce | flops 1280 | bytes 10240 | tf_op jit(solution)/shard_map/psum | solution.py:125
  259.7 2.1 fusion.41
  261.8 155.5 %reduce-scatter.5.cloned.1.call-done = bf16[48,3,16,128]{3,2,1,0:T(8,128)(2,1)} async-done(((bf16[768,3,16,128]{3,2,1,0:T(8,128)(2,1)}), bf16[48,3,16,128]{3,2,1,0:T(8,128)(2,1)}) %reduce-scatter.5.cloned.1.call-update) | async-done | bytes 589840 | tf_op jit(solution)/shard_map/reduce_scatter | solution.py:102
  417.3 1.2 copy.50
  418.4 1.1 convert_element_type.144
  (34 shorter events, 0.4 us)
Async XLA Ops:
  8.0 95.9 %copy-start = (bf16[256,256]{1,0:T(8,128)(2,1)S(1)}, bf16[256,256]{1,0:T(8,128)(2,1)}, u32[]{:S(2)}) copy-start(bf16[256,256]{1,0:T(8,128)(2,1)} %param.9) | copy-start | bytes 393220
  8.0 195.0 %all-reduce.7.cloned.1.call-start = ((), (), s32[]{:S(2)}) async-start(), calls=%async_computation.1 | async-start | bytes 786432 | tf_op jit(solution)/shard_map/psum | solution.py:116
  30.8 71.0 %copy-start.6 = (u32[256]{0:T(256)S(1)}, u32[256]{0:T(256)}, u32[]{:S(2)}) copy-start(u32[256]{0:T(256)} %constant.62) | copy-start | bytes 3076
  103.2 0.7 copy-start.2
  104.1 3.2 copy-start.3
  109.1 7.2 %collective-permute-start = (bf16[2,3,256,128]{3,2,0,1:T(8,128)(2,1)S(1)}, bf16[2,3,256,128]{3,2,0,1:T(8,128)(2,1)S(1)}, u32[]{:S(2)}, u32[]{:S(2)}) collective-permute-start(bf16[2,3,256,128]{3,2,0,1:T(8,128)(2,1)S(1)} %pad_maximum_fusion), channel_id=1, source_target_pairs={{0,2},{2,4},{4,6},{6,8},{8,10},{10,12},{12,14},{14,0},{1,3},{3,5},... | collective-permute-start | bytes 1179656 | tf_op jit(solution)/shard_map/ppermute | solution.py:95
  116.3 7.2 %collective-permute-start.1 = (bf16[2,3,256,128]{3,2,0,1:T(8,128)(2,1)S(1)}, bf16[2,3,256,128]{3,2,0,1:T(8,128)(2,1)S(1)}, u32[]{:S(2)}, u32[]{:S(2)}) collective-permute-start(bf16[2,3,256,128]{3,2,0,1:T(8,128)(2,1)S(1)} %collective-permute-done), channel_id=1, source_target_pairs={{0,2},{2,4},{4,6},{6,8},{8,10},{10,12},{12,14},{14,0},{1,3},{3,5},... | collective-permute-start | bytes 1179656 | tf_op jit(solution)/shard_map/ppermute | solution.py:95
  116.3 7.2 %collective-permute-start.4 = (bf16[2,3,256,128]{3,2,0,1:T(8,128)(2,1)S(1)}, bf16[2,3,256,128]{3,2,0,1:T(8,128)(2,1)S(1)}, u32[]{:S(2)}, u32[]{:S(2)}) collective-permute-start(bf16[2,3,256,128]{3,2,0,1:T(8,128)(2,1)S(1)} %pad_maximum_fusion), channel_id=1, source_target_pairs={{0,14},{2,0},{4,2},{6,4},{8,6},{10,8},{12,10},{14,12},{1,15},{3,1}... | collective-permute-start | bytes 1179656 | tf_op jit(solution)/shard_map/ppermute | solution.py:97
  123.5 7.2 %collective-permute-start.2 = (bf16[2,3,256,128]{3,2,0,1:T(8,128)(2,1)S(1)}, bf16[2,3,256,128]{3,2,0,1:T(8,128)(2,1)S(1)}, u32[]{:S(2)}, u32[]{:S(2)}) collective-permute-start(bf16[2,3,256,128]{3,2,0,1:T(8,128)(2,1)S(1)} %collective-permute-done.1), channel_id=1, source_target_pairs={{0,2},{2,4},{4,6},{6,8},{8,10},{10,12},{12,14},{14,0},{1,3},{3,5},... | collective-permute-start | bytes 1179656 | tf_op jit(solution)/shard_map/ppermute | solution.py:95
  123.5 7.3 %collective-permute-start.5 = (bf16[2,3,256,128]{3,2,0,1:T(8,128)(2,1)S(1)}, bf16[2,3,256,128]{3,2,0,1:T(8,128)(2,1)S(1)}, u32[]{:S(2)}, u32[]{:S(2)}) collective-permute-start(bf16[2,3,256,128]{3,2,0,1:T(8,128)(2,1)S(1)} %collective-permute-done.4), channel_id=1, source_target_pairs={{0,14},{2,0},{4,2},{6,4},{8,6},{10,8},{12,10},{14,12},{1,15},{3,1}... | collective-permute-start | bytes 1179656 | tf_op jit(solution)/shard_map/ppermute | solution.py:97
  130.7 7.2 %collective-permute-start.3 = (bf16[2,3,256,128]{3,2,0,1:T(8,128)(2,1)S(1)}, bf16[2,3,256,128]{3,2,0,1:T(8,128)(2,1)S(1)}, u32[]{:S(2)}, u32[]{:S(2)}) collective-permute-start(bf16[2,3,256,128]{3,2,0,1:T(8,128)(2,1)S(1)} %collective-permute-done.2), channel_id=1, source_target_pairs={{0,2},{2,4},{4,6},{6,8},{8,10},{10,12},{12,14},{14,0},{1,3},{3,5},... | collective-permute-start | bytes 1179656 | tf_op jit(solution)/shard_map/ppermute | solution.py:95
  130.8 7.5 %collective-permute-start.6 = (bf16[2,3,256,128]{3,2,0,1:T(8,128)(2,1)S(1)}, bf16[2,3,256,128]{3,2,0,1:T(8,128)(2,1)S(1)}, u32[]{:S(2)}, u32[]{:S(2)}) collective-permute-start(bf16[2,3,256,128]{3,2,0,1:T(8,128)(2,1)S(1)} %collective-permute-done.5), channel_id=1, source_target_pairs={{0,14},{2,0},{4,2},{6,4},{8,6},{10,8},{12,10},{14,12},{1,15},{3,1}... | collective-permute-start | bytes 1179656 | tf_op jit(solution)/shard_map/ppermute | solution.py:97
  138.9 2.7 copy-start.4
  141.5 7.5 %copy-start.1 = (bf16[256,768]{1,0:T(8,128)(2,1)S(1)}, bf16[256,768]{1,0:T(8,128)(2,1)}, u32[]{:S(2)}) copy-start(bf16[256,768]{1,0:T(8,128)(2,1)} %param.5) | copy-start | bytes 1179652
  141.5 7.5 %copy-start.5 = (f32[768]{0:T(1024)S(1)}, f32[768]{0:T(1024)}, u32[]{:S(2)}) copy-start(f32[768]{0:T(1024)} %param.6) | copy-start | bytes 9220
  148.8 268.4 %reduce-scatter.5.cloned.1.call-start = ((), (), s32[]{:S(2)}) async-start(), calls=%async_computation.2 | async-start | bytes 10027008 | tf_op jit(solution)/shard_map/reduce_scatter | solution.py:102
Sparse Core Ops, SparseCore 0:
  148.9 54.0 all-reduce.6
Sparse Core Ops, SparseCore 1:
  170.7 246.5 reduce-scatter.4
